TPU v7x, 32 devices: a whole 2x2x4 slice. The times are simulated.
32 devices in a mesh: seq: 4 (over z), head: 4 (over y, x), dp: 2 (over core).
Axes of the slice: x: 2, y: 2, z: 4, core: 2. Of those that a mesh axis runs over, the one named last changes fastest.
Arguments:
- inputs: bfloat16 [4096, 4096], P(('dp', 'seq'), 'head'), parts along dimension 0, may hold values from -2 to 2
- step_raw: float32 [4096, 64], P(('dp', 'seq'), 'head'), parts along dimension 0, may hold values from -5 to 600
- decay_rate: float32 [64], P('head'), may hold values from 0.002 to 0.1
- skip_gain: float32 [64], P('head'), may hold values from 0.3 to 3
- b_proj: bfloat16 [4096, 8, 256], P(('dp', 'seq')), parts along dimension 0, may hold values from -2 to 2
- c_proj: bfloat16 [4096, 8, 256], P(('dp', 'seq')), parts along dimension 0, may hold values from -2 to 2
- lengths: int32 [4], P('dp'), parts along dimension 0, may hold values from 1 to 512, as said below
- cotangent: bfloat16 [4096, 4096], P(('dp', 'seq'), 'head'), parts along dimension 0, may hold values from -1.5 to 1.5
Outputs:
- outputs: bfloat16 [4096, 4096], P(('dp', 'seq'), 'head'), parts along dimension 0
- grad_inputs: bfloat16 [4096, 4096], P(('dp', 'seq'), 'head'), parts along dimension 0
- grad_step: float32 [4096, 64], P(('dp', 'seq'), 'head'), parts along dimension 0
- grad_b: float32 [4096, 8, 256], P(('dp', 'seq', 'head')), parts along dimension 0
- grad_c: float32 [4096, 8, 256], P(('dp', 'seq', 'head')), parts along dimension 0
There are 2 independent parts, one for each index of `dp`. A program takes and returns all parts, laid end to end along the dimension named above; an argument that names none is the same for every part. Nothing has to cross between parts.
Inputs may be any that keep to these rules, and one draw needn't show every extreme that they name: `lengths`: some response has exactly 512 tokens.
All inputs are finite; a program needn't handle non-finite values.
Results may differ from a plain program's by a relative error of at most 0.009.
Values sent between devices are 32-bit elements; how exact they have to be, the bound alone decides.
A program may use at most 128 MiB of HBM per device.

v0:
```python
import functools

import jax
import jax.numpy as jnp
from jax import lax
from jax.experimental import pallas as pl
from jax.experimental.pallas import tpu as pltpu
from jax.sharding import PartitionSpec as P

BLOCK = 256
PREFIX_DEVS = 2
LANES = 128
F32 = jnp.float32
BF16 = jnp.bfloat16
EXACT = lax.Precision.HIGHEST


def mm(a, b, ca, cb):
    return lax.dot_general(a, b, (((ca,), (cb,)), ((), ())), preferred_element_type=F32)


def layer_kernel(
    peers, heads, groups,
    x_ref, dy_ref, b_ref, c_ref, small_ref, gain_ref, decay_ref,
    y_ref, dx_ref, gs_ref, db_ref, dc_ref,
    wi_b, dt_b, wi_t, dt_t, state, first_state, grad_own, later_grad,
    state_in, state_out, grad_in, grad_out, y_acc, dx_acc, q_acc, mask_b,
    fs_sem, fr_sem, bs_sem, br_sem,
):
    pos = lax.axis_index("seq")
    prefix = jnp.where(pos < PREFIX_DEVS, 1.0, 0.0).astype(F32)
    rows = x_ref.shape[0]
    blocks = rows // BLOCK
    pairs = groups // 2
    half = groups * 64
    low = lax.broadcasted_iota(jnp.int32, (1, LANES), 1) < 64

    barrier = pltpu.get_barrier_semaphore()

    @pl.when(pos > 0)
    def _():
        pl.semaphore_signal(barrier, inc=1, device_id={"seq": pos - 1}, device_id_type=pl.DeviceIdType.MESH)

    @pl.when(pos < peers - 1)
    def _():
        pl.semaphore_signal(barrier, inc=1, device_id={"seq": pos + 1}, device_id_type=pl.DeviceIdType.MESH)

    tri = lax.broadcasted_iota(jnp.int32, (BLOCK, BLOCK), 0) >= lax.broadcasted_iota(
        jnp.int32, (BLOCK, BLOCK), 1
    )

    def span(k):
        return slice(k * BLOCK, (k + 1) * BLOCK)

    for k in range(blocks):
        vals = small_ref[span(k), :]
        sums = lax.dot_general(
            tri.astype(F32), vals, (((1,), (0,)), ((), ())),
            preferred_element_type=F32, precision=EXACT,
        )
        wi_t[:, span(k)] = sums.T
        dt_t[:, span(k)] = vals.T
        for h in range(heads):
            wi_b[h, span(k), :] = jnp.broadcast_to(sums[:, heads + h : heads + h + 1], (BLOCK, LANES))
            dt_b[h, span(k), :] = jnp.broadcast_to(vals[:, h : h + 1], (BLOCK, LANES))
        mask_b[span(k), :] = jnp.broadcast_to(vals[:, 3 * heads : 3 * heads + 1], (BLOCK, LANES))

    def turn(v):
        return pltpu.roll(v, 64, 1)

    def slabs(ref, p):
        lo = ref[:, pl.ds(pl.multiple_of(p * LANES, LANES), LANES)].astype(F32)
        hi = ref[:, pl.ds(pl.multiple_of(half + p * LANES, LANES), LANES)].astype(F32)
        return lo, hi

    def join(lo, hi):
        return jnp.where(low, lo, turn(hi)), jnp.where(low, turn(lo), hi)

    def by_head(ref, g, k):
        return jnp.where(low, ref[g, span(k), :], ref[groups + g, span(k), :])

    def total(g, k):
        at = pl.ds((k + 1) * BLOCK - 1, 1)
        return jnp.where(low, wi_b[g, at, :], wi_b[groups + g, at, :])

    def hop_f(p):
        part = pl.ds(2 * p, 2)
        return pltpu.make_async_remote_copy(
            src_ref=state_out.at[part], dst_ref=state_in.at[part],
            send_sem=fs_sem.at[p], recv_sem=fr_sem.at[p],
            device_id={"seq": pos + 1}, device_id_type=pl.DeviceIdType.MESH,
        )

    def hop_b(p):
        part = pl.ds(2 * p, 2)
        return pltpu.make_async_remote_copy(
            src_ref=grad_out.at[part], dst_ref=grad_in.at[part],
            send_sem=bs_sem.at[p], recv_sem=br_sem.at[p],
            device_id={"seq": pos - 1}, device_id_type=pl.DeviceIdType.MESH,
        )

    def whole(g):
        return jnp.exp(prefix * (total(g, 0) + total(g, 1)))

    def pass_f(p):
        for j in range(2):
            g = 2 * p + j
            state_out[g] = whole(g) * state_in[g] + prefix * state[g]
        hop_f(p).start()

    def pass_b(p):
        for j in range(2):
            g = 2 * p + j
            grad_out[g] = whole(g) * grad_in[g] + grad_own[g]
        hop_b(p).start()

    @pl.when(pos == 0)
    def _():
        state_in[...] = jnp.zeros_like(state_in)

    @pl.when(pos == peers - 1)
    def _():
        grad_in[...] = jnp.zeros_like(grad_in)

    @pl.when(jnp.logical_or(pos == 0, pos == peers - 1))
    def _():
        pl.semaphore_wait(barrier, 1)

    @pl.when(jnp.logical_and(pos > 0, pos < peers - 1))
    def _():
        pl.semaphore_wait(barrier, 2)

    def local_states(p, carry):
        xs = join(*slabs(x_ref, p))
        dys = join(*slabs(dy_ref, p))
        for j in range(2):
            g = 2 * p + j
            adds, backs = [], []
            for k in range(blocks):
                wi = by_head(wi_b, g, k)
                dt = by_head(dt_b, g, k)
                scaled = (xs[j][span(k)] * (dt * jnp.exp(total(g, k) - wi))).astype(BF16)
                adds.append(mm(b_ref[g, span(k), :], scaled, 0, 0))
                lifted = (dys[j][span(k)] * mask_b[span(k), :] * jnp.exp(wi)).astype(BF16)
                backs.append(mm(c_ref[g, span(k), :], lifted, 0, 0))
            first_state[g] = adds[0]
            state[g] = jnp.exp(total(g, 1)) * adds[0] + adds[1]
            later_grad[g] = backs[1]
            grad_own[g] = backs[0] + jnp.exp(total(g, 0)) * backs[1]

        @pl.when(pos == 0)
        def _():
            pass_f(p)

        @pl.when(pos == peers - 1)
        def _():
            pass_b(p)

        return carry

    lax.fori_loop(0, pairs, local_states, 0)

    def inside(p, carry):
        xs = join(*slabs(x_ref, p))
        dys = join(*slabs(dy_ref, p))
        for j in range(2):
            g = 2 * p + j
            for k in range(blocks):
                b_blk = b_ref[g, span(k), :]
                c_blk = c_ref[g, span(k), :]
                scores = mm(c_blk, b_blk, 1, 1)
                x16 = xs[j][span(k)].astype(BF16)
                dyf = dys[j][span(k)] * mask_b[span(k), :]
                dy16 = dyf.astype(BF16)
                ys, dxs = [], []
                d_scores = None
                for m in range(2):
                    h = m * groups + g
                    col = wi_b[h, span(k), :]
                    col = jnp.concatenate([col, col], axis=1)
                    row = wi_t[pl.ds(heads + h, 1), span(k)]
                    decay = jnp.where(tri, jnp.exp(jnp.minimum(col - row, 0.0)), 0.0)
                    decay = decay * dt_t[pl.ds(h, 1), span(k)]
                    weights = (scores * decay).astype(BF16)
                    mine = low if m == 0 else jnp.logical_not(low)
                    dy_m = jnp.where(mine, dyf, 0.0).astype(BF16)
                    d_weights = mm(dy_m, x16, 1, 1) * decay
                    d_scores = d_weights if d_scores is None else d_scores + d_weights
                    ys.append(mm(weights, x16, 1, 0))
                    dxs.append(mm(weights, dy16, 0, 0))
                y_acc[g, span(k), :] = jnp.where(low, ys[0], ys[1])
                dx_acc[g, span(k), :] = jnp.where(low, dxs[0], dxs[1])
                ds16 = d_scores.astype(BF16)
                dc_ref[g, span(k), :] = mm(ds16, b_blk, 1, 0)
                db_ref[g, span(k), :] = mm(ds16, c_blk, 0, 0)

        @pl.when(jnp.logical_and(pos > 0, pos < peers - 1))
        def _():
            hop_f(p).wait_recv()
            pass_f(p)
            hop_b(p).wait_recv()
            pass_b(p)

        return carry

    lax.fori_loop(0, pairs, inside, 0)

    q_acc[...] = jnp.zeros_like(q_acc)
    last = lax.broadcasted_iota(jnp.int32, (BLOCK, 1), 0) == BLOCK - 1
    pick_row = lax.broadcasted_iota(jnp.int32, (4 * LANES, LANES), 0)
    pick_col = lax.broadcasted_iota(jnp.int32, (4 * LANES, LANES), 1)
    pick_head = (
        jnp.where(pick_row % LANES >= 64, groups, 0) + jnp.where(pick_row >= 2 * LANES, heads, 0)
    )

    def across(p, carry):
        @pl.when(pos == peers - 1)
        def _():
            hop_f(p).wait_recv()

        @pl.when(pos == 0)
        def _():
            hop_b(p).wait_recv()

        xs = join(*slabs(x_ref, p))
        dys = join(*slabs(dy_ref, p))
        gain_lo = gain_ref[:, pl.ds(pl.multiple_of(p * LANES, LANES), LANES)]
        gain_hi = gain_ref[:, pl.ds(pl.multiple_of(half + p * LANES, LANES), LANES)]
        gains = join(gain_lo, gain_hi)
        y_parts, dx_parts = [], []
        for j in range(2):
            g = 2 * p + j
            pick = (pick_col == pick_head + g).astype(BF16)
            start = state_in[g]
            carry_grad = prefix * grad_in[g]
            entered = (start, jnp.exp(total(g, 0)) * start + first_state[g])
            leaving = (later_grad[g] + jnp.exp(total(g, 1)) * carry_grad, carry_grad)
            y_rows, dx_rows = [], []
            for k in range(blocks):
                wi = by_head(wi_b, g, k)
                dt = by_head(dt_b, g, k)
                end = total(g, k)
                up = jnp.exp(wi)
                down = dt * jnp.exp(end - wi)
                e16 = entered[k].astype(BF16)
                g16 = leaving[k].astype(BF16)
                x = xs[j][span(k)]
                mask = mask_b[span(k), :]
                dy = dys[j][span(k)] * mask
                b_blk = b_ref[g, span(k), :]
                c_blk = c_ref[g, span(k), :]
                y = y_acc[g, span(k), :] + up * mm(c_blk, e16, 1, 0)
                dx_s = down * mm(b_blk, g16, 1, 0)
                dx = dx_acc[g, span(k), :] + dx_s
                dc_ref[g, span(k), :] += mm((dy * up).astype(BF16), e16, 1, 1)
                db_ref[g, span(k), :] += mm((x * down).astype(BF16), g16, 1, 1)
                q2 = x * dx
                extra = jnp.sum(x * dx_s, axis=0, keepdims=True) + jnp.exp(end) * jnp.sum(
                    leaving[k] * entered[k], axis=0, keepdims=True
                )
                q1 = dy * y - q2 + jnp.where(last, extra, 0.0)
                q1h = q1.astype(BF16)
                q2h = q2.astype(BF16)
                q1l = (q1 - q1h.astype(F32)).astype(BF16)
                q2l = (q2 - q2h.astype(F32)).astype(BF16)
                q_acc[span(k), :] += mm(jnp.concatenate([q1h, q1l, q2h, q2l], axis=1), pick, 1, 0)
                y_rows.append((y + gains[j] * x) * mask)
                dx_rows.append(dx + gains[j] * dy)
            y_parts.append(jnp.concatenate(y_rows, axis=0))
            dx_parts.append(jnp.concatenate(dx_rows, axis=0))
        for ref, parts in ((y_ref, y_parts), (dx_ref, dx_parts)):
            lo, hi = join(*parts)
            ref[:, pl.ds(pl.multiple_of(p * LANES, LANES), LANES)] = lo.astype(BF16)
            ref[:, pl.ds(pl.multiple_of(half + p * LANES, LANES), LANES)] = hi.astype(BF16)
        return carry

    lax.fori_loop(0, pairs, across, 0)

    for k in range(blocks):
        vals = small_ref[span(k), :]
        q = q_acc[span(k), :]
        d_log = lax.dot_general(
            tri.astype(F32), q, (((0,), (0,)), ((), ())),
            preferred_element_type=F32, precision=EXACT,
        )
        d_step = pltpu.roll(q, LANES - heads, 1)
        slope = pltpu.roll(vals, LANES - 2 * heads, 1)
        safe = jnp.where(vals > 0.0, vals, 1.0)
        gs_ref[span(k), :] = slope * (d_step / safe - decay_ref[...] * d_log)

    def finish(p, carry):
        @pl.when(pos < peers - 1)
        def _():
            hop_f(p).wait_send()

        @pl.when(pos > 0)
        def _():
            hop_b(p).wait_send()

        return carry

    lax.fori_loop(0, pairs, finish, 0)


def on_device(inputs, step_raw, decay_rate, skip_gain, b_proj, c_proj, lengths, cotangent):
    rows, width = inputs.shape
    heads = decay_rate.shape[0]
    groups, states = b_proj.shape[1:]
    peers = lax.axis_size("seq")
    position = lax.axis_index("seq")
    is_prefix = position < PREFIX_DEVS
    mine = lax.dynamic_slice_in_dim(lengths, jnp.maximum(position - PREFIX_DEVS, 0), 1)
    ids = jnp.arange(rows, dtype=jnp.int32)
    mask = jnp.where(jnp.logical_or(is_prefix, ids < mine[0]), 1.0, 0.0).astype(F32)[:, None]
    step = jax.nn.softplus(step_raw) * mask
    small = jnp.concatenate(
        [step, -(step * decay_rate[None, :]), jax.nn.sigmoid(step_raw) * mask,
         jnp.broadcast_to(mask, (rows, LANES - 3 * heads))], axis=1
    )
    gain = jnp.repeat(skip_gain, width // heads)[None, :]
    decay = jnp.pad(decay_rate, (0, LANES - heads))[None, :]
    b_lead = jnp.swapaxes(b_proj, 0, 1)
    c_lead = jnp.swapaxes(c_proj, 0, 1)
    vmem = pl.BlockSpec(memory_space=pltpu.VMEM)
    carry = pltpu.VMEM((groups, states, LANES), F32)
    dma = pltpu.SemaphoreType.DMA((groups // 2,))

    y, dx, gs, db, dc = pl.pallas_call(
        functools.partial(layer_kernel, peers, heads, groups),
        out_shape=(
            jax.ShapeDtypeStruct((rows, width), BF16),
            jax.ShapeDtypeStruct((rows, width), BF16),
            jax.ShapeDtypeStruct((rows, LANES), F32),
            jax.ShapeDtypeStruct((groups, rows, states), F32),
            jax.ShapeDtypeStruct((groups, rows, states), F32),
        ),
        in_specs=[vmem] * 7,
        out_specs=(vmem,) * 5,
        scratch_shapes=[
            pltpu.VMEM((heads, rows, LANES), F32),
            pltpu.VMEM((heads, rows, LANES), F32),
            pltpu.VMEM((LANES, rows), F32),
            pltpu.VMEM((LANES, rows), F32),
            carry, carry, carry, carry, carry, carry, carry, carry,
            pltpu.VMEM((groups, rows, LANES), F32),
            pltpu.VMEM((groups, rows, LANES), F32),
            pltpu.VMEM((rows, LANES), F32),
            pltpu.VMEM((rows, LANES), F32),
            dma, dma, dma, dma,
        ],
        compiler_params=pltpu.CompilerParams(
            collective_id=0, has_side_effects=True, vmem_limit_bytes=56 * 1024 * 1024
        ),
    )(inputs, cotangent, b_lead, c_lead, small, gain, decay)
    db = lax.psum_scatter(db, "head", scatter_dimension=1, tiled=True)
    dc = lax.psum_scatter(dc, "head", scatter_dimension=1, tiled=True)
    return (y, dx, gs[:, :heads], jnp.swapaxes(db, 0, 1), jnp.swapaxes(dc, 0, 1))


def solution(mesh):
    rows = P(("dp", "seq"), "head")
    proj = P(("dp", "seq"), None, None)
    grads = P(("dp", "seq", "head"), None, None)
    return jax.shard_map(
        on_device,
        mesh=mesh,
        in_specs=(rows, rows, P("head"), P("head"), proj, proj, P("dp"), rows),
        out_specs=(rows, rows, rows, grads, grads),
        check_vma=False,
    )
```

profile of v0, /device:TPU:0, one launch (start us, length us, event | category | flops | bytes accessed | tf_op | source)
XLA Modules:
  0.0 216.5 jit_solution(7341311208035184517)
XLA Ops:
  7.2 0.0 reduce-scatter.3.cloned.1.call-start
  7.2 1.2 pad_bitcast_fusion.decay_ref
  8.4 0.7 broadcast_in_dim.24
  9.1 0.7 broadcast_in_dim_reshape.3.gain_ref
  9.8 0.9 copy.26
  10.7 1.2 dynamic_slice.3
  11.9 0.6 fusion.2
  12.6 0.9 multiply_negate_fusion
  13.4 5.1 %copy_bitcast_fusion = (bf16[8,512,256]{2,1,0:T(8,128)(2,1)}, bf16[8,512,256]{2,1,0:T(8,128)(2,1)}) fusion(bf16[512,8,256]{2,1,0:T(8,128)(2,1)} %param.13, bf16[512,8,256]{2,1,0:T(8,128)(2,1)} %param.12), kind=kLoop, calls=%fused_computation | loop fusion | bytes 8388608 | tf_op jit(solution)/shard_map/transpose | solution.py:323
  18.6 0.1 broadcast_in_dim.23
  18.7 1.0 pad_maximum_fusion.small_ref
  19.7 79.5 %shard_map.119 = (bf16[512,1024]{1,0:T(8,128)(2,1)}, bf16[512,1024]{1,0:T(8,128)(2,1)}, f32[512,128]{1,0:T(8,128)}, f32[8,512,256]{2,1,0:T(8,128)}, f32[8,512,256]{2,1,0:T(8,128)}) custom-call(bf16[512,1024]{1,0:T(8,128)(2,1)} %x_ref.1, bf16[512,1024]{1,0:T(8,128)(2,1)} %dy_ref.1, bf16[8,512,256]{2,1,0:T(8,128)(2,1)} %get-tuple-element.29.b_ref, ...), custom_call_target="tpu_custom_call" | custom-call | tf_op jit(solution)/shard_map/pallas_call | solution.py:328
  99.2 0.0 reduce-scatter.3.cloned.1.call-update
  99.2 0.0 reduce-scatter.5.cloned.1.call-start
  99.2 0.0 copy-start.2
  99.2 0.7 reduce-scatter.5.cloned.1.call-update
  99.9 0.2 copy-done.2
  100.2 0.7 copy.35
  100.9 48.0 %reduce-scatter.3.cloned.1.call-done = f32[8,128,256]{2,1,0:T(8,128)} async-done(((f32[8,512,256]{2,1,0:T(8,128)}), f32[8,128,256]{2,1,0:T(8,128)}) %reduce-scatter.3.cloned.1.call-update) | async-done | bytes 1048592 | tf_op jit(solution)/shard_map/reduce_scatter | solution.py:355
  148.9 0.0 copy-start.1
  148.9 2.9 %copy.36 = f32[128,8,256]{2,1,0:T(8,128)} copy(f32[128,8,256]{2,0,1:T(8,128)} %bitcast.10) | data formatting | bytes 2097152
  151.8 53.1 %reduce-scatter.5.cloned.1.call-done = f32[8,128,256]{2,1,0:T(8,128)} async-done(((f32[8,512,256]{2,1,0:T(8,128)}), f32[8,128,256]{2,1,0:T(8,128)}) %reduce-scatter.5.cloned.1.call-update) | async-done | bytes 1048592 | tf_op jit(solution)/shard_map/reduce_scatter | solution.py:356
  204.9 0.0 copy-start
  204.9 2.9 %copy.37 = f32[128,8,256]{2,1,0:T(8,128)} copy(f32[128,8,256]{2,0,1:T(8,128)} %bitcast.11) | data formatting | bytes 2097152
  207.8 0.0 copy-done.1
  207.8 1.0 copy.43
  208.7 0.0 copy-done
  208.7 1.0 copy.44
Async XLA Ops:
  7.2 141.7 %reduce-scatter.3.cloned.1.call-start = ((), (), s32[]{:S(2)}) async-start(), calls=%async_computation.2 | async-start | bytes 5242880 | tf_op jit(solution)/shard_map/reduce_scatter | solution.py:355
  99.2 105.7 %reduce-scatter.5.cloned.1.call-start = ((), (), s32[]{:S(2)}) async-start(), calls=%async_computation.3 | async-start | bytes 5242880 | tf_op jit(solution)/shard_map/reduce_scatter | solution.py:356
  99.2 1.0 copy-start.2
  148.9 58.9 %copy-start.1 = (bf16[512,1024]{1,0:T(8,128)(2,1)S(1)}, bf16[512,1024]{1,0:T(8,128)(2,1)}, u32[]{:S(2)}) copy-start(bf16[512,1024]{1,0:T(8,128)(2,1)} %get-tuple-element.35) | copy-start | bytes 3145732
  204.9 3.9 %copy-start = (bf16[512,1024]{1,0:T(8,128)(2,1)S(1)}, bf16[512,1024]{1,0:T(8,128)(2,1)}, u32[]{:S(2)}) copy-start(bf16[512,1024]{1,0:T(8,128)(2,1)} %get-tuple-element.36) | copy-start | bytes 3145732
Sparse Core Ops, SparseCore 0:
  99.3 49.5 reduce-scatter.2
  152.1 52.6 reduce-scatter.4
where the time goes:
time: 217 us
  waiting for transfers between devices  102 us (47%)
  Pallas kernels  79.5 us (37%)
  local copies, waits for them, and re-layouts  18.6 us (9%)
  between operations  14.1 us (6%)
  other arithmetic  2.51 us (1%)
    pallas_call x1, Pallas kernels, on_device(): pl.pallas_call(functools.partial(layer_kernel, peers, heads, groups), out...  79.5 us
    reduce_scatter x1, waiting for transfers between devices, on_device(): dc = lax.psum_scatter(dc, 'head', scatter_dimension=1, tiled=True)  53.1 us
    reduce_scatter x1, waiting for transfers between devices, on_device(): db = lax.psum_scatter(db, 'head', scatter_dimension=1, tiled=True)  48 us
    unnamed x12, local copies, waits for them, and re-layouts  9.58 us
    transpose x1, local copies, waits for them, and re-layouts, on_device(): c_lead = jnp.swapaxes(c_proj, 0, 1)  5.13 us
  transfers between devices with their start and end apart: 2, of which 2 were waited for; matrix products, arithmetic and copies ran while one was open for 2% of the time, Pallas kernels for 0%

commit v1 on v0

--- a/solution.py
+++ b/solution.py
@@ -20,14 +20,15 @@
 
 
 def layer_kernel(
-    peers, heads, groups,
+    peers, ranks, heads, groups,
     x_ref, dy_ref, b_ref, c_ref, small_ref, gain_ref, decay_ref,
-    y_ref, dx_ref, gs_ref, db_ref, dc_ref,
+    y_ref, dx_ref, gs_ref, db_out, dc_out,
     wi_b, dt_b, wi_t, dt_t, state, first_state, grad_own, later_grad,
     state_in, state_out, grad_in, grad_out, y_acc, dx_acc, q_acc, mask_b,
-    fs_sem, fr_sem, bs_sem, br_sem,
+    parts, arrived, fs_sem, fr_sem, bs_sem, br_sem, ps_sem, pr_sem,
 ):
     pos = lax.axis_index("seq")
+    rank = lax.axis_index("head")
     prefix = jnp.where(pos < PREFIX_DEVS, 1.0, 0.0).astype(F32)
     rows = x_ref.shape[0]
     blocks = rows // BLOCK
@@ -35,7 +36,13 @@
     half = groups * 64
     low = lax.broadcasted_iota(jnp.int32, (1, LANES), 1) < 64
 
+    share = rows // ranks
     barrier = pltpu.get_barrier_semaphore()
+    for away in range(1, ranks):
+        pl.semaphore_signal(
+            barrier, inc=1, device_id={"head": lax.rem(rank + away, ranks)},
+            device_id_type=pl.DeviceIdType.MESH,
+        )
 
     @pl.when(pos > 0)
     def _():
@@ -99,6 +106,15 @@
             device_id={"seq": pos - 1}, device_id_type=pl.DeviceIdType.MESH,
         )
 
+    def give(g, away):
+        to = lax.rem(rank + away, ranks)
+        return pltpu.make_async_remote_copy(
+            src_ref=parts.at[g, :, pl.ds(pl.multiple_of(to * share, share), share), :],
+            dst_ref=arrived.at[away - 1, g],
+            send_sem=ps_sem.at[away - 1, g], recv_sem=pr_sem.at[away - 1, g],
+            device_id={"head": to}, device_id_type=pl.DeviceIdType.MESH,
+        )
+
     def whole(g):
         return jnp.exp(prefix * (total(g, 0) + total(g, 1)))
 
@@ -124,11 +140,11 @@
 
     @pl.when(jnp.logical_or(pos == 0, pos == peers - 1))
     def _():
-        pl.semaphore_wait(barrier, 1)
+        pl.semaphore_wait(barrier, ranks)
 
     @pl.when(jnp.logical_and(pos > 0, pos < peers - 1))
     def _():
-        pl.semaphore_wait(barrier, 2)
+        pl.semaphore_wait(barrier, ranks + 1)
 
     def local_states(p, carry):
         xs = join(*slabs(x_ref, p))
@@ -160,7 +176,7 @@
 
     lax.fori_loop(0, pairs, local_states, 0)
 
-    def inside(p, carry):
+    def inside(p):
         xs = join(*slabs(x_ref, p))
         dys = join(*slabs(dy_ref, p))
         for j in range(2):
@@ -191,19 +207,8 @@
                 y_acc[g, span(k), :] = jnp.where(low, ys[0], ys[1])
                 dx_acc[g, span(k), :] = jnp.where(low, dxs[0], dxs[1])
                 ds16 = d_scores.astype(BF16)
-                dc_ref[g, span(k), :] = mm(ds16, b_blk, 1, 0)
-                db_ref[g, span(k), :] = mm(ds16, c_blk, 0, 0)
-
-        @pl.when(jnp.logical_and(pos > 0, pos < peers - 1))
-        def _():
-            hop_f(p).wait_recv()
-            pass_f(p)
-            hop_b(p).wait_recv()
-            pass_b(p)
-
-        return carry
-
-    lax.fori_loop(0, pairs, inside, 0)
+                parts[g, 1, span(k), :] = mm(ds16, b_blk, 1, 0)
+                parts[g, 0, span(k), :] = mm(ds16, c_blk, 0, 0)
 
     q_acc[...] = jnp.zeros_like(q_acc)
     last = lax.broadcasted_iota(jnp.int32, (BLOCK, 1), 0) == BLOCK - 1
@@ -213,7 +218,7 @@
         jnp.where(pick_row % LANES >= 64, groups, 0) + jnp.where(pick_row >= 2 * LANES, heads, 0)
     )
 
-    def across(p, carry):
+    def across(p):
         @pl.when(pos == peers - 1)
         def _():
             hop_f(p).wait_recv()
@@ -252,8 +257,8 @@
                 y = y_acc[g, span(k), :] + up * mm(c_blk, e16, 1, 0)
                 dx_s = down * mm(b_blk, g16, 1, 0)
                 dx = dx_acc[g, span(k), :] + dx_s
-                dc_ref[g, span(k), :] += mm((dy * up).astype(BF16), e16, 1, 1)
-                db_ref[g, span(k), :] += mm((x * down).astype(BF16), g16, 1, 1)
+                parts[g, 1, span(k), :] += mm((dy * up).astype(BF16), e16, 1, 1)
+                parts[g, 0, span(k), :] += mm((x * down).astype(BF16), g16, 1, 1)
                 q2 = x * dx
                 extra = jnp.sum(x * dx_s, axis=0, keepdims=True) + jnp.exp(end) * jnp.sum(
                     leaving[k] * entered[k], axis=0, keepdims=True
@@ -266,15 +271,43 @@
                 q_acc[span(k), :] += mm(jnp.concatenate([q1h, q1l, q2h, q2l], axis=1), pick, 1, 0)
                 y_rows.append((y + gains[j] * x) * mask)
                 dx_rows.append(dx + gains[j] * dy)
+            for away in range(1, ranks):
+                give(g, away).start()
             y_parts.append(jnp.concatenate(y_rows, axis=0))
             dx_parts.append(jnp.concatenate(dx_rows, axis=0))
-        for ref, parts in ((y_ref, y_parts), (dx_ref, dx_parts)):
-            lo, hi = join(*parts)
+        for ref, pair in ((y_ref, y_parts), (dx_ref, dx_parts)):
+            lo, hi = join(*pair)
             ref[:, pl.ds(pl.multiple_of(p * LANES, LANES), LANES)] = lo.astype(BF16)
             ref[:, pl.ds(pl.multiple_of(half + p * LANES, LANES), LANES)] = hi.astype(BF16)
+
+    lag = max(1, peers - 3)
+    middle = jnp.logical_and(pos > 0, pos < peers - 1)
+
+    def stage(s, carry):
+        pf = s - (pos - 1)
+        pb = s - (peers - 2 - pos)
+
+        @pl.when(jnp.logical_and(middle, jnp.logical_and(pf >= 0, pf < pairs)))
+        def _():
+            hop_f(pf).wait_recv()
+            pass_f(pf)
+
+        @pl.when(jnp.logical_and(middle, jnp.logical_and(pb >= 0, pb < pairs)))
+        def _():
+            hop_b(pb).wait_recv()
+            pass_b(pb)
+
+        @pl.when(s < pairs)
+        def _():
+            inside(s)
+
+        @pl.when(jnp.logical_and(s >= lag, s < pairs + lag))
+        def _():
+            across(s - lag)
+
         return carry
 
-    lax.fori_loop(0, pairs, across, 0)
+    lax.fori_loop(0, pairs + lag, stage, 0)
 
     for k in range(blocks):
         vals = small_ref[span(k), :]
@@ -288,6 +321,20 @@
         safe = jnp.where(vals > 0.0, vals, 1.0)
         gs_ref[span(k), :] = slope * (d_step / safe - decay_ref[...] * d_log)
 
+    own = pl.ds(pl.multiple_of(rank * share, share), share)
+    for g in range(groups):
+        db = parts[g, 0, own, :]
+        dc = parts[g, 1, own, :]
+        for away in range(1, ranks):
+            give(g, away).wait_recv()
+            db = db + arrived[away - 1, g, 0]
+            dc = dc + arrived[away - 1, g, 1]
+        db_out[:, g, :] = db
+        dc_out[:, g, :] = dc
+    for g in range(groups):
+        for away in range(1, ranks):
+            give(g, away).wait_send()
+
     def finish(p, carry):
         @pl.when(pos < peers - 1)
         def _():
@@ -307,6 +354,7 @@
     heads = decay_rate.shape[0]
     groups, states = b_proj.shape[1:]
     peers = lax.axis_size("seq")
+    ranks = lax.axis_size("head")
     position = lax.axis_index("seq")
     is_prefix = position < PREFIX_DEVS
     mine = lax.dynamic_slice_in_dim(lengths, jnp.maximum(position - PREFIX_DEVS, 0), 1)
@@ -326,13 +374,13 @@
     dma = pltpu.SemaphoreType.DMA((groups // 2,))
 
     y, dx, gs, db, dc = pl.pallas_call(
-        functools.partial(layer_kernel, peers, heads, groups),
+        functools.partial(layer_kernel, peers, ranks, heads, groups),
         out_shape=(
             jax.ShapeDtypeStruct((rows, width), BF16),
             jax.ShapeDtypeStruct((rows, width), BF16),
             jax.ShapeDtypeStruct((rows, LANES), F32),
-            jax.ShapeDtypeStruct((groups, rows, states), F32),
-            jax.ShapeDtypeStruct((groups, rows, states), F32),
+            jax.ShapeDtypeStruct((rows // ranks, groups, states), F32),
+            jax.ShapeDtypeStruct((rows // ranks, groups, states), F32),
         ),
         in_specs=[vmem] * 7,
         out_specs=(vmem,) * 5,
@@ -346,15 +394,17 @@
             pltpu.VMEM((groups, rows, LANES), F32),
             pltpu.VMEM((rows, LANES), F32),
             pltpu.VMEM((rows, LANES), F32),
+            pltpu.VMEM((groups, 2, rows, states), F32),
+            pltpu.VMEM((ranks - 1, groups, 2, rows // ranks, states), F32),
             dma, dma, dma, dma,
+            pltpu.SemaphoreType.DMA((ranks - 1, groups)),
+            pltpu.SemaphoreType.DMA((ranks - 1, groups)),
         ],
         compiler_params=pltpu.CompilerParams(
             collective_id=0, has_side_effects=True, vmem_limit_bytes=56 * 1024 * 1024
         ),
     )(inputs, cotangent, b_lead, c_lead, small, gain, decay)
-    db = lax.psum_scatter(db, "head", scatter_dimension=1, tiled=True)
-    dc = lax.psum_scatter(dc, "head", scatter_dimension=1, tiled=True)
-    return (y, dx, gs[:, :heads], jnp.swapaxes(db, 0, 1), jnp.swapaxes(dc, 0, 1))
+    return (y, dx, gs[:, :heads], db, dc)
 
 
 def solution(mesh):

time: 217 us -> 143 us (0.66)
  waiting for transfers between devices: 102 us -> 0 us
  Pallas kernels: 79.5 us -> 123 us
  between operations: 14.1 us -> 0.7 us
    reduce_scatter x2 -> x0, waiting for transfers between devices: 101 us -> none  [the longest x1 53.1 us: on_device(): dc = lax.psum_scatter(dc, 'head', scatter_dimension=1, tiled=True)]
    pallas_call x1, Pallas kernels: 79.5 us -> 123 us  [on_device(): pl.pallas_call(functools.partial(layer_kernel, peers, ranks, heads, group...]
    unnamed x12 -> x14, local copies, waits for them, and re-layouts: 9.58 us -> 7.92 us
  transfers between devices with their start and end apart: 2 -> 0, of which waited for: 2 -> 0; matrix products, arithmetic and copies ran while one was open for 2% -> 0% of each run, Pallas kernels for 0% -> 0%
where the time goes in v1:
time: 143 us; the launch traced here: 142 us
  Pallas kernels  123 us (86%)
  local copies, waits for them, and re-layouts  16.5 us (12%)
  other arithmetic  2.51 us (2%)
    pallas_call x1, Pallas kernels, on_device(): pl.pallas_call(functools.partial(layer_kernel, peers, ranks, heads, group...  123 us
    unnamed x14, local copies, waits for them, and re-layouts  7.92 us
    transpose x1, local copies, waits for them, and re-layouts, on_device(): c_lead = jnp.swapaxes(c_proj, 0, 1)  4.47 us

profile of v1, /device:TPU:0, one launch (start us, length us, event | category | flops | bytes accessed | tf_op | source)
XLA Modules:
  0.0 142.2 jit_solution(13971363002583047089)
XLA Ops:
  0.6 0.0 copy-start
  0.6 1.4 dynamic_slice.3
  2.0 1.2 pad_bitcast_fusion.decay_ref
  3.2 0.6 fusion.2
  3.9 0.7 broadcast_in_dim.24
  4.6 0.7 broadcast_in_dim_reshape.3.gain_ref
  5.3 0.1 broadcast_in_dim.23
  5.4 0.9 copy.24
  6.3 0.9 multiply_negate_fusion
  7.2 1.0 pad_maximum_fusion.small_ref
  8.1 0.0 copy-done
  8.1 4.5 %copy_bitcast_fusion = (bf16[8,512,256]{2,1,0:T(8,128)(2,1)}, bf16[8,512,256]{2,1,0:T(8,128)(2,1)}) fusion(bf16[512,8,256]{2,1,0:T(8,128)(2,1)S(1)} %copy-done, bf16[512,8,256]{2,1,0:T(8,128)(2,1)} %param.12), kind=kLoop, calls=%fused_computation | loop fusion | bytes 8388608 | tf_op jit(solution)/shard_map/transpose | solution.py:371
  12.6 122.6 %shard_map.119 = (bf16[512,1024]{1,0:T(8,128)(2,1)}, bf16[512,1024]{1,0:T(8,128)(2,1)}, f32[512,128]{1,0:T(8,128)}, f32[128,8,256]{2,1,0:T(8,128)}, f32[128,8,256]{2,1,0:T(8,128)}) custom-call(bf16[512,1024]{1,0:T(8,128)(2,1)} %x_ref.1, bf16[512,1024]{1,0:T(8,128)(2,1)} %dy_ref.1, bf16[8,512,256]{2,1,0:T(8,128)(2,1)} %get-tuple-element.29.b_ref, ...), custom_call_target="tpu_custom_call" | custom-call | tf_op jit(solution)/shard_map/pallas_call | solution.py:376
  135.2 0.0 copy-start.3
  135.2 1.8 %copy.33 = f32[512,16]{0,1:T(8,128)} copy(f32[512,16]{1,0:T(8,128)} %bitcast.8) | data formatting | bytes 65536
  137.0 0.0 copy-start.2
  137.0 2.4 %copy.41 = bf16[512,1024]{1,0:T(8,128)(2,1)} copy(bf16[512,1024]{1,0:T(8,128)(2,1)} %get-tuple-element.35) | data formatting | bytes 2097152
  139.3 0.0 copy-done.3
  139.3 0.0 copy-start.1
  139.3 1.0 copy.42
  140.3 0.0 copy-done.2
  140.3 1.0 copy.43
  141.3 0.0 copy-done.1
  141.3 1.0 copy.44
Async XLA Ops:
  0.6 7.5 %copy-start = (bf16[512,8,256]{2,1,0:T(8,128)(2,1)S(1)}, bf16[512,8,256]{2,1,0:T(8,128)(2,1)}, u32[]{:S(2)}) copy-start(bf16[512,8,256]{2,1,0:T(8,128)(2,1)} %param.13) | copy-start | bytes 6291460
  135.2 4.1 %copy-start.3 = (bf16[512,1024]{1,0:T(8,128)(2,1)S(1)}, bf16[512,1024]{1,0:T(8,128)(2,1)}, u32[]{:S(2)}) copy-start(bf16[512,1024]{1,0:T(8,128)(2,1)} %get-tuple-element.36) | copy-start | bytes 3145732
  137.0 3.3 %copy-start.2 = (f32[128,8,256]{2,1,0:T(8,128)S(1)}, f32[128,8,256]{2,1,0:T(8,128)}, u32[]{:S(2)}) copy-start(f32[128,8,256]{2,1,0:T(8,128)} %get-tuple-element.38) | copy-start | bytes 3145732
  139.3 1.9 %copy-start.1 = (f32[128,8,256]{2,1,0:T(8,128)S(1)}, f32[128,8,256]{2,1,0:T(8,128)}, u32[]{:S(2)}) copy-start(f32[128,8,256]{2,1,0:T(8,128)} %get-tuple-element.39) | copy-start | bytes 3145732

commit v2 on v1

--- a/solution.py
+++ b/solution.py
@@ -21,11 +21,11 @@
 
 def layer_kernel(
     peers, ranks, heads, groups,
-    x_ref, dy_ref, b_ref, c_ref, small_ref, gain_ref, decay_ref,
+    x_ref, dy_ref, b_ref, c_ref, step_ref, gain_ref, decay_ref, lengths_ref,
     y_ref, dx_ref, gs_ref, db_out, dc_out,
     wi_b, dt_b, wi_t, dt_t, state, first_state, grad_own, later_grad,
-    state_in, state_out, grad_in, grad_out, y_acc, dx_acc, q_acc, mask_b,
-    parts, arrived, fs_sem, fr_sem, bs_sem, br_sem, ps_sem, pr_sem,
+    state_in, state_out, grad_in, grad_out, y_acc, dx_acc, q_acc, mask_b, gain_b, decay_b,
+    parts, arrived, summed, fs_sem, fr_sem, bs_sem, br_sem, ps_sem, pr_sem, ss_sem, sr_sem,
 ):
     pos = lax.axis_index("seq")
     rank = lax.axis_index("head")
@@ -59,18 +59,33 @@
     def span(k):
         return slice(k * BLOCK, (k + 1) * BLOCK)
 
+    limit = jnp.where(pos < PREFIX_DEVS, rows, lengths_ref[jnp.maximum(pos - PREFIX_DEVS, 0)])
+    ids = lax.broadcasted_iota(jnp.int32, (1, BLOCK), 1)
+    for h in range(heads):
+        gain_b[h : h + 1, :] = jnp.full((1, LANES), gain_ref[h], F32)
+        decay_b[h : h + 1, :] = jnp.full((1, LANES), decay_ref[h], F32)
+    rate = jnp.concatenate([decay_b[...]] * (BLOCK // LANES), axis=1)
+
+    def kept(k):
+        return jnp.where(ids + k * BLOCK < limit, 1.0, 0.0).astype(F32)
+
     for k in range(blocks):
-        vals = small_ref[span(k), :]
+        raw = step_ref[:, span(k)]
+        keep = kept(k)
+        step = (jnp.maximum(raw, 0.0) + jnp.log1p(jnp.exp(-jnp.abs(raw)))) * keep
         sums = lax.dot_general(
-            tri.astype(F32), vals, (((1,), (0,)), ((), ())),
+            -(step * rate), tri.astype(F32), (((1,), (1,)), ((), ())),
             preferred_element_type=F32, precision=EXACT,
         )
-        wi_t[:, span(k)] = sums.T
-        dt_t[:, span(k)] = vals.T
+        wi_t[:, span(k)] = sums
+        dt_t[:, span(k)] = step
+        tall = jnp.concatenate(
+            [step, sums, jnp.broadcast_to(keep, (LANES - 2 * heads, BLOCK))], axis=0
+        ).T
         for h in range(heads):
-            wi_b[h, span(k), :] = jnp.broadcast_to(sums[:, heads + h : heads + h + 1], (BLOCK, LANES))
-            dt_b[h, span(k), :] = jnp.broadcast_to(vals[:, h : h + 1], (BLOCK, LANES))
-        mask_b[span(k), :] = jnp.broadcast_to(vals[:, 3 * heads : 3 * heads + 1], (BLOCK, LANES))
+            wi_b[h, span(k), :] = jnp.broadcast_to(tall[:, heads + h : heads + h + 1], (BLOCK, LANES))
+            dt_b[h, span(k), :] = jnp.broadcast_to(tall[:, h : h + 1], (BLOCK, LANES))
+        mask_b[span(k), :] = jnp.broadcast_to(tall[:, 2 * heads : 2 * heads + 1], (BLOCK, LANES))
 
     def turn(v):
         return pltpu.roll(v, 64, 1)
@@ -114,6 +129,79 @@
             send_sem=ps_sem.at[away - 1, g], recv_sem=pr_sem.at[away - 1, g],
             device_id={"head": to}, device_id_type=pl.DeviceIdType.MESH,
         )
+
+    def piece(g, kind, owner):
+        return parts.at[g, kind, pl.ds(pl.multiple_of(owner * share, share), share), :]
+
+    def flip(bit):
+        low_bit = lax.rem(rank, 2)
+        if bit == 1:
+            return rank + 1 - 2 * low_bit
+        if bit == 2:
+            return lax.rem(rank + 2, 4)
+        return lax.rem(rank + 2, 4) + 1 - 2 * low_bit
+
+    def first_hop(g, kind, which):
+        to = flip(kind + 1)
+        return pltpu.make_async_remote_copy(
+            src_ref=piece(g, kind, to if which == 0 else flip(3)),
+            dst_ref=arrived.at[which, g, kind],
+            send_sem=ps_sem.at[2 * kind + which, g], recv_sem=pr_sem.at[2 * kind + which, g],
+            device_id={"head": to}, device_id_type=pl.DeviceIdType.MESH,
+        )
+
+    def second_hop(g, kind):
+        to = flip(2 - kind)
+        return pltpu.make_async_remote_copy(
+            src_ref=piece(g, kind, to), dst_ref=summed.at[g, kind],
+            send_sem=ss_sem.at[kind, g], recv_sem=sr_sem.at[kind, g],
+            device_id={"head": to}, device_id_type=pl.DeviceIdType.MESH,
+        )
+
+    square = ranks == 4
+
+    def send_group(g):
+        if square:
+            for which in (1, 0):
+                for kind in range(2):
+                    first_hop(g, kind, which).start()
+        else:
+            for away in range(1, ranks):
+                give(g, away).start()
+
+    def forward_group(g):
+        if square:
+            for kind in range(2):
+                first_hop(g, kind, 1).wait_recv()
+                at = pl.ds(pl.multiple_of(flip(2 - kind) * share, share), share)
+                parts[g, kind, at, :] += arrived[1, g, kind]
+                second_hop(g, kind).start()
+
+    def collect_group(g):
+        own = pl.ds(pl.multiple_of(rank * share, share), share)
+        for kind, out in enumerate((db_out, dc_out)):
+            val = parts[g, kind, own, :]
+            if square:
+                first_hop(g, kind, 0).wait_recv()
+                second_hop(g, kind).wait_recv()
+                val = val + arrived[0, g, kind] + summed[g, kind]
+            else:
+                if kind == 0:
+                    for away in range(1, ranks):
+                        give(g, away).wait_recv()
+                for away in range(1, ranks):
+                    val = val + arrived[away - 1, g, kind]
+            out[:, g, :] = val
+
+    def settle_group(g):
+        if square:
+            for kind in range(2):
+                for which in range(2):
+                    first_hop(g, kind, which).wait_send()
+                second_hop(g, kind).wait_send()
+        else:
+            for away in range(1, ranks):
+                give(g, away).wait_send()
 
     def whole(g):
         return jnp.exp(prefix * (total(g, 0) + total(g, 1)))
@@ -194,7 +282,7 @@
                     h = m * groups + g
                     col = wi_b[h, span(k), :]
                     col = jnp.concatenate([col, col], axis=1)
-                    row = wi_t[pl.ds(heads + h, 1), span(k)]
+                    row = wi_t[pl.ds(h, 1), span(k)]
                     decay = jnp.where(tri, jnp.exp(jnp.minimum(col - row, 0.0)), 0.0)
                     decay = decay * dt_t[pl.ds(h, 1), span(k)]
                     weights = (scores * decay).astype(BF16)
@@ -229,13 +317,11 @@
 
         xs = join(*slabs(x_ref, p))
         dys = join(*slabs(dy_ref, p))
-        gain_lo = gain_ref[:, pl.ds(pl.multiple_of(p * LANES, LANES), LANES)]
-        gain_hi = gain_ref[:, pl.ds(pl.multiple_of(half + p * LANES, LANES), LANES)]
-        gains = join(gain_lo, gain_hi)
         y_parts, dx_parts = [], []
         for j in range(2):
             g = 2 * p + j
             pick = (pick_col == pick_head + g).astype(BF16)
+            gain = jnp.where(low, gain_b[pl.ds(g, 1), :], gain_b[pl.ds(groups + g, 1), :])
             start = state_in[g]
             carry_grad = prefix * grad_in[g]
             entered = (start, jnp.exp(total(g, 0)) * start + first_state[g])
@@ -269,10 +355,9 @@
                 q1l = (q1 - q1h.astype(F32)).astype(BF16)
                 q2l = (q2 - q2h.astype(F32)).astype(BF16)
                 q_acc[span(k), :] += mm(jnp.concatenate([q1h, q1l, q2h, q2l], axis=1), pick, 1, 0)
-                y_rows.append((y + gains[j] * x) * mask)
-                dx_rows.append(dx + gains[j] * dy)
-            for away in range(1, ranks):
-                give(g, away).start()
+                y_rows.append((y + gain * x) * mask)
+                dx_rows.append(dx + gain * dy)
+            send_group(g)
             y_parts.append(jnp.concatenate(y_rows, axis=0))
             dx_parts.append(jnp.concatenate(dx_rows, axis=0))
         for ref, pair in ((y_ref, y_parts), (dx_ref, dx_parts)):
@@ -305,35 +390,32 @@
         def _():
             across(s - lag)
 
+        @pl.when(jnp.logical_and(s > lag, s < pairs + lag))
+        def _():
+            for j in range(2):
+                forward_group(2 * (s - lag - 1) + j)
+
         return carry
 
     lax.fori_loop(0, pairs + lag, stage, 0)
+    for g in range(groups - 2, groups):
+        forward_group(g)
 
     for k in range(blocks):
-        vals = small_ref[span(k), :]
-        q = q_acc[span(k), :]
+        q = q_acc[span(k), :].T
+        step = dt_t[:, span(k)]
         d_log = lax.dot_general(
-            tri.astype(F32), q, (((0,), (0,)), ((), ())),
+            q[:heads], tri.astype(F32), (((1,), (0,)), ((), ())),
             preferred_element_type=F32, precision=EXACT,
         )
-        d_step = pltpu.roll(q, LANES - heads, 1)
-        slope = pltpu.roll(vals, LANES - 2 * heads, 1)
-        safe = jnp.where(vals > 0.0, vals, 1.0)
-        gs_ref[span(k), :] = slope * (d_step / safe - decay_ref[...] * d_log)
-
-    own = pl.ds(pl.multiple_of(rank * share, share), share)
+        slope = jax.nn.sigmoid(step_ref[:, span(k)]) * kept(k)
+        safe = jnp.where(step > 0.0, step, 1.0)
+        gs_ref[:, span(k)] = slope * (q[heads : 2 * heads] / safe - rate * d_log)
+
     for g in range(groups):
-        db = parts[g, 0, own, :]
-        dc = parts[g, 1, own, :]
-        for away in range(1, ranks):
-            give(g, away).wait_recv()
-            db = db + arrived[away - 1, g, 0]
-            dc = dc + arrived[away - 1, g, 1]
-        db_out[:, g, :] = db
-        dc_out[:, g, :] = dc
+        collect_group(g)
     for g in range(groups):
-        for away in range(1, ranks):
-            give(g, away).wait_send()
+        settle_group(g)
 
     def finish(p, carry):
         @pl.when(pos < peers - 1)
@@ -355,21 +437,11 @@
     groups, states = b_proj.shape[1:]
     peers = lax.axis_size("seq")
     ranks = lax.axis_size("head")
-    position = lax.axis_index("seq")
-    is_prefix = position < PREFIX_DEVS
-    mine = lax.dynamic_slice_in_dim(lengths, jnp.maximum(position - PREFIX_DEVS, 0), 1)
-    ids = jnp.arange(rows, dtype=jnp.int32)
-    mask = jnp.where(jnp.logical_or(is_prefix, ids < mine[0]), 1.0, 0.0).astype(F32)[:, None]
-    step = jax.nn.softplus(step_raw) * mask
-    small = jnp.concatenate(
-        [step, -(step * decay_rate[None, :]), jax.nn.sigmoid(step_raw) * mask,
-         jnp.broadcast_to(mask, (rows, LANES - 3 * heads))], axis=1
-    )
-    gain = jnp.repeat(skip_gain, width // heads)[None, :]
-    decay = jnp.pad(decay_rate, (0, LANES - heads))[None, :]
+    hops = 2 if ranks == 4 else ranks - 1
     b_lead = jnp.swapaxes(b_proj, 0, 1)
     c_lead = jnp.swapaxes(c_proj, 0, 1)
     vmem = pl.BlockSpec(memory_space=pltpu.VMEM)
+    smem = pl.BlockSpec(memory_space=pltpu.SMEM)
     carry = pltpu.VMEM((groups, states, LANES), F32)
     dma = pltpu.SemaphoreType.DMA((groups // 2,))
 
@@ -378,33 +450,40 @@
         out_shape=(
             jax.ShapeDtypeStruct((rows, width), BF16),
             jax.ShapeDtypeStruct((rows, width), BF16),
-            jax.ShapeDtypeStruct((rows, LANES), F32),
+            jax.ShapeDtypeStruct((heads, rows), F32),
             jax.ShapeDtypeStruct((rows // ranks, groups, states), F32),
             jax.ShapeDtypeStruct((rows // ranks, groups, states), F32),
         ),
-        in_specs=[vmem] * 7,
+        in_specs=[vmem] * 5 + [smem] * 3,
         out_specs=(vmem,) * 5,
         scratch_shapes=[
             pltpu.VMEM((heads, rows, LANES), F32),
             pltpu.VMEM((heads, rows, LANES), F32),
-            pltpu.VMEM((LANES, rows), F32),
-            pltpu.VMEM((LANES, rows), F32),
+            pltpu.VMEM((heads, rows), F32),
+            pltpu.VMEM((heads, rows), F32),
             carry, carry, carry, carry, carry, carry, carry, carry,
             pltpu.VMEM((groups, rows, LANES), F32),
             pltpu.VMEM((groups, rows, LANES), F32),
             pltpu.VMEM((rows, LANES), F32),
             pltpu.VMEM((rows, LANES), F32),
+            pltpu.VMEM((heads, LANES), F32),
+            pltpu.VMEM((heads, LANES), F32),
             pltpu.VMEM((groups, 2, rows, states), F32),
-            pltpu.VMEM((ranks - 1, groups, 2, rows // ranks, states), F32),
+            pltpu.VMEM((hops, groups, 2, rows // ranks, states), F32),
+            pltpu.VMEM((groups, 2, rows // ranks, states), F32),
             dma, dma, dma, dma,
-            pltpu.SemaphoreType.DMA((ranks - 1, groups)),
-            pltpu.SemaphoreType.DMA((ranks - 1, groups)),
+            pltpu.SemaphoreType.DMA((max(ranks - 1, 4), groups)),
+            pltpu.SemaphoreType.DMA((max(ranks - 1, 4), groups)),
+            pltpu.SemaphoreType.DMA((2, groups)),
+            pltpu.SemaphoreType.DMA((2, groups)),
         ],
         compiler_params=pltpu.CompilerParams(
             collective_id=0, has_side_effects=True, vmem_limit_bytes=56 * 1024 * 1024
         ),
-    )(inputs, cotangent, b_lead, c_lead, small, gain, decay)
-    return (y, dx, gs[:, :heads], db, dc)
+    )(
+        inputs, cotangent, b_lead, c_lead, step_raw.T, skip_gain, decay_rate, lengths
+    )
+    return (y, dx, gs.T, db, dc)
 
 
 def solution(mesh):

time: 143 us -> 112 us (0.78)
  Pallas kernels: 123 us -> 100 us
  local copies, waits for them, and re-layouts: 16.5 us -> 11 us
  other arithmetic: 2.51 us -> 0 us
    pallas_call x1, Pallas kernels: 123 us -> 100 us  [on_device(): pl.pallas_call(functools.partial(layer_kernel, peers, ranks, heads, group...]
    broadcast_in_dim x3 -> x0, local copies, waits for them, and re-layouts: 2.01 us -> none  [the longest x1 1.17 us: on_device(): decay = jnp.pad(decay_rate, (0, LANES - heads))[None, :]]
    unnamed x14 -> x13, local copies, waits for them, and re-layouts: 7.92 us -> 5.95 us
where the time goes in v2:
time: 112 us
  Pallas kernels  100 us (89%)
  local copies, waits for them, and re-layouts  11 us (10%)
    pallas_call x1, Pallas kernels, on_device(): pl.pallas_call(functools.partial(layer_kernel, peers, ranks, heads, group...  100 us
    unnamed x13, local copies, waits for them, and re-layouts  5.95 us
    transpose x1, local copies, waits for them, and re-layouts, on_device(): c_lead = jnp.swapaxes(c_proj, 0, 1)  5.09 us

profile of v2, /device:TPU:0, one launch (start us, length us, event | category | flops | bytes accessed | tf_op | source)
XLA Modules:
  0.0 112.0 jit_solution(17644785182277552058)
XLA Ops:
  0.6 5.1 %copy_bitcast_fusion = (bf16[8,512,256]{2,1,0:T(8,128)(2,1)}, bf16[8,512,256]{2,1,0:T(8,128)(2,1)}) fusion(bf16[512,8,256]{2,1,0:T(8,128)(2,1)} %param.13, bf16[512,8,256]{2,1,0:T(8,128)(2,1)} %param.12), kind=kLoop, calls=%fused_computation | loop fusion | bytes 8388608 | tf_op jit(solution)/shard_map/transpose | solution.py:442
  5.7 100.3 %shard_map.119 = (bf16[512,1024]{1,0:T(8,128)(2,1)}, bf16[512,1024]{1,0:T(8,128)(2,1)}, f32[16,512]{1,0:T(8,128)}, f32[128,8,256]{2,1,0:T(8,128)}, f32[128,8,256]{2,1,0:T(8,128)}) custom-call(bf16[512,1024]{1,0:T(8,128)(2,1)} %x_ref.1, bf16[512,1024]{1,0:T(8,128)(2,1)} %dy_ref.1, bf16[8,512,256]{2,1,0:T(8,128)(2,1)} %get-tuple-element.16.b_ref, ...), custom_call_target="tpu_custom_call" | custom-call | tf_op jit(solution)/shard_map/pallas_call | solution.py:448
  106.1 0.0 copy-start.2
  106.1 0.0 copy-start.3
  106.1 0.0 copy-start.1
  106.1 2.4 %copy.22 = bf16[512,1024]{1,0:T(8,128)(2,1)} copy(bf16[512,1024]{1,0:T(8,128)(2,1)} %get-tuple-element.22) | data formatting | bytes 2097152
  108.5 0.0 copy-done.2
  108.5 0.0 copy-start
  108.5 1.0 copy.23
  109.5 0.0 copy-done.3
  109.5 0.6 copy.24
  110.1 0.0 copy-done.1
  110.1 1.0 copy.25
  111.1 0.0 copy-done
  111.1 1.0 copy.26
Async XLA Ops:
  106.1 2.4 %copy-start.2 = (bf16[512,1024]{1,0:T(8,128)(2,1)S(1)}, bf16[512,1024]{1,0:T(8,128)(2,1)}, u32[]{:S(2)}) copy-start(bf16[512,1024]{1,0:T(8,128)(2,1)} %get-tuple-element.23) | copy-start | bytes 3145732
  106.1 3.4 %copy-start.3 = (f32[16,512]{1,0:T(8,128)S(1)}, f32[16,512]{1,0:T(8,128)}, u32[]{:S(2)}) copy-start(f32[16,512]{1,0:T(8,128)} %get-tuple-element.12) | copy-start | bytes 98308
  106.1 4.0 %copy-start.1 = (f32[128,8,256]{2,1,0:T(8,128)S(1)}, f32[128,8,256]{2,1,0:T(8,128)}, u32[]{:S(2)}) copy-start(f32[128,8,256]{2,1,0:T(8,128)} %get-tuple-element.25) | copy-start | bytes 3145732
  108.5 2.6 %copy-start = (f32[128,8,256]{2,1,0:T(8,128)S(1)}, f32[128,8,256]{2,1,0:T(8,128)}, u32[]{:S(2)}) copy-start(f32[128,8,256]{2,1,0:T(8,128)} %get-tuple-element.26) | copy-start | bytes 3145732
